TPU v7x, 32 devices: a whole 2x2x4 slice. The times are simulated.
32 devices in a mesh: groups: 2 (over x), blk: 8 (over z, y), dp: 2 (over core).
Axes of the slice: x: 2, y: 2, z: 4, core: 2. Of those that a mesh axis runs over, the one named last changes fastest.
Arguments:
- particles: bfloat16 [32768, 4096], P(('groups', 'blk', 'dp')), parts along dimension 0, may hold values from -44 to 44
- defocus: int32 [32768], P(('groups', 'blk', 'dp')), parts along dimension 0, may hold values from 0 to 15
- pick_dest: int32 [32768, 1], P(('groups', 'blk', 'dp')), parts along dimension 0, may hold values from 0 to 15; in each aligned block of 1024 rows (0 to 1023, 1024 to 2047, ...) at most 128 rows name the same one
- references: bfloat16 [192, 4096], P(('groups', 'blk')), parts along dimension 0, may hold values from -4 to 4
- ctf_table: float32 [32, 4096], P('groups'), parts along dimension 0, may hold values from 0.1 to 1
Outputs:
- weighted_sums: float32 [192, 4096], P(('groups', 'blk', 'dp')), parts along dimension 0
- ctf_weights: float32 [192, 4096], P(('groups', 'blk', 'dp')), parts along dimension 0
- posterior: float32 [65536, 96], P(('groups', 'blk', 'dp')), parts along dimension 0
There are 2 independent parts, one for each index of `groups`. A program takes and returns all parts, laid end to end along the dimension named above; each array names one. Nothing has to cross between parts.
Inputs may be any that keep to these rules, and one draw needn't show every extreme that they name: `pick_dest`: of the particles that one device holds, at most 128 name any one destination, and in every draw some device sends exactly 128 to one destination.
All inputs are finite; a program needn't handle non-finite values.
Results may differ from a plain program's by a relative error of at most 0.0028.
Values may be sent and summed in bfloat16 or wider, within the bound.
A program may use at most 128 MiB of HBM per device.

v0:
```python
import math
import jax
import jax.numpy as jnp
from jax import lax
from jax.sharding import PartitionSpec as P

PIX = 4096


def lookup(class_ids, table_rows):
    return (class_ids[:, None] == jnp.arange(table_rows, dtype=jnp.int32)[None, :]).astype(
        jnp.float32
    )


def per_device(particles, defocus, pick_dest, references, ctf_table):
    held_rows = particles.shape[0]
    table_rows = ctf_table.shape[0]
    kr_total = references.shape[0] * lax.axis_size("blk")
    device_count = lax.axis_size(("blk", "dp"))
    capacity = max(2, 2 * held_rows // device_count)
    recv_rows = device_count * capacity
    rows_mine = kr_total // device_count
    score_scale = 1.0 / math.sqrt(PIX)
    ctf_square = ctf_table * ctf_table
    own_onehot = lookup(defocus, table_rows)
    modulation = jnp.dot(own_onehot, ctf_table, precision=lax.Precision.HIGHEST)
    modulated = (particles.astype(jnp.float32) * modulation).astype(jnp.bfloat16)
    destination = pick_dest[:, 0]
    dest_hot = (destination[:, None] == jnp.arange(device_count, dtype=jnp.int32)[None, :]).astype(
        jnp.int32
    )
    earlier = jnp.cumsum(dest_hot, axis=0) - dest_hot
    ranking = jnp.sum(earlier * dest_hot, axis=1)
    slot_index = destination * capacity + ranking
    ref_piece = lax.all_gather(references, "blk", axis=0, tiled=True)
    cross_term = lax.dot_general(
        modulated, ref_piece, (((1,), (1,)), ((), ())), preferred_element_type=jnp.float32
    )
    piece_float = ref_piece.astype(jnp.float32)
    quadratic = 0.5 * lax.dot_general(
        ctf_square,
        piece_float * piece_float,
        (((1,), (1,)), ((), ())),
        precision=lax.Precision.HIGHEST,
    )
    scores = score_scale * (
        cross_term - jnp.dot(own_onehot, quadratic, precision=lax.Precision.HIGHEST)
    )
    largest = jnp.max(scores, axis=1, keepdims=True)
    exponent = jnp.exp(scores - largest)
    weights = exponent / jnp.sum(exponent, axis=1, keepdims=True)
    send_weights = jnp.zeros((recv_rows, kr_total), jnp.float32).at[slot_index].set(weights)
    posterior = lax.all_to_all(send_weights, ("blk", "dp"), split_axis=0, concat_axis=0, tiled=True)
    weights_low = weights.astype(jnp.bfloat16)
    weighted_sums = lax.psum_scatter(
        lax.dot_general(
            weights_low, modulated, (((0,), (0,)), ((), ())), preferred_element_type=jnp.float32
        ),
        ("blk", "dp"),
        scatter_dimension=0,
        tiled=True,
    )
    class_sums = lax.dot_general(
        own_onehot, weights, (((0,), (0,)), ((), ())), precision=lax.Precision.HIGHEST
    )
    totals = lax.psum(class_sums, ("blk", "dp"))
    own_sums = lax.dynamic_slice_in_dim(
        totals, lax.axis_index(("blk", "dp")) * rows_mine, rows_mine, 1
    )
    ctf_weights = lax.dot_general(
        own_sums, ctf_square, (((0,), (0,)), ((), ())), precision=lax.Precision.HIGHEST
    )
    return (weighted_sums, ctf_weights, posterior)


def solution(mesh):
    placed = (
        P(("groups", "blk", "dp"), None),
        P(("groups", "blk", "dp")),
        P(("groups", "blk", "dp"), None),
        P(("groups", "blk"), None),
        P("groups", None),
    )
    return jax.shard_map(
        per_device,
        mesh=mesh,
        in_specs=placed,
        out_specs=(
            P(("groups", "blk", "dp"), None),
            P(("groups", "blk", "dp"), None),
            P(("groups", "blk", "dp"), None),
        ),
        check_vma=False,
    )
```

profile of v0, /device:TPU:0, one launch (start us, length us, event | category | flops | bytes accessed | tf_op | source)
XLA Modules:
  0.0 189.7 jit_solution(3554859009608589075)
XLA Ops:
  0.6 34.8 %all-gather = bf16[8,12,4096]{2,1,0:T(8,128)(2,1)S(1)} all-gather(bf16[1,12,4096]{2,1,0:T(8,128)(2,1)} %bitcast.40), channel_id=1, replica_groups=mesh['groups'=2,'blk'=8,'dp'=2] {'blk'}, dimensions={0}, use_global_device_ids=true | all-gather | bytes 884736 | tf_op jit(solution)/shard_map/all_gather | solution.py:36
  35.4 0.2 reshape.38
  35.6 2.3 %fusion.5 = f32[16,96]{1,0:T(8,128)S(1)} fusion(bf16[96,4096]{1,0:T(8,128)(2,1)S(1)} %reshape.38, f32[16,4096]{1,0:T(8,128)} %param.9), kind=kOutput, calls=%fused_computation.7 | convolution fusion | flops 76350976 | bytes 1054720 | tf_op jit(solution)/shard_map/dot_general | solution.py:41
  37.9 9.8 %multiply_convert_fusion = bf16[1024,4096]{1,0:T(8,128)(2,1)S(1)} fusion(bf16[1024,4096]{1,0:T(8,128)(2,1)} %param.5, f32[16,4096]{1,0:T(8,128)} %param.9, s32[1024]{0:T(1024)} %param.6), kind=kOutput, calls=%fused_computation.1 | convolution fusion | flops 817905664 | bytes 17043456 | tf_op jit(solution)/shard_map/dot_general | solution.py:27
  47.7 0.0 copy-start
  47.7 3.2 %copy-done = bf16[1024,4096]{1,0:T(8,128)(2,1)} copy-done((bf16[1024,4096]{1,0:T(8,128)(2,1)}, bf16[1024,4096]{1,0:T(8,128)(2,1)S(1)}, u32[]{:S(2)}) %copy-start) | copy-done | bytes 8388632
  51.0 0.0 copy-start.2
  51.0 0.0 copy-start.3
  51.0 2.7 %fusion.28 = f32[1024,96]{0,1:T(8,128)S(1)} fusion(bf16[1024,4096]{1,0:T(8,128)(2,1)S(1)} %multiply_convert_fusion, bf16[96,4096]{1,0:T(8,128)(2,1)S(1)} %reshape.38), kind=kOutput, calls=%fused_computation.37 | convolution fusion | flops 805306368 | bytes 9568256 | tf_op jit(solution)/shard_map/dot_general | solution.py:37
  53.7 0.0 copy-done.2
  53.7 0.6 fusion.27
  54.3 0.1 fusion.12
  54.3 0.1 fusion.11
  54.4 0.2 copy.20
  54.6 0.0 copy-done.3
  54.6 4.5 %reduce-window.6 = s32[16,8,128]{2,1,0:T(8,128)S(1)} reduce-window(s32[16,8,128]{2,1,0:T(8,128)S(1)} %fusion.24, s32[]{:T(128)} %constant.6.clone.1), window={size=1x1x128 pad=0_0x0_0x127_0}, to_apply=%region_4.5 | reduce-window | flops 2080768 | bytes 131076 | tf_op jit(solution)/shard_map/reduce-window
  59.2 0.1 slice.8
  59.2 0.1 copy.18
  59.4 0.1 copy.19
  59.5 0.1 broadcast_add_fusion
  59.6 3.3 %scatter_custom_fusion = f32[2048,96]{1,0:T(8,128)S(1)} fusion(s32[1024]{0:T(1024)S(1)} %bitcast.45, f32[1024,96]{1,0:T(8,128)S(1)} %copy.20, f32[]{:T(128)} %constant.15.clone.1), kind=kCustom, calls=%fused_computation.9 | custom fusion | bytes 786436 | tf_op jit(solution)/shard_map/scatter | solution.py:53
  63.0 1.2 copy.21
  64.2 5.5 %all-to-all-start = ((f32[16,128,96]{1,2,0:T(8,128)}), f32[16,128,96]{1,2,0:T(8,128)S(1)}, u32[]{:S(2)}, u32[]{:S(2)}) async-start(f32[16,128,96]{1,2,0:T(8,128)} %copy.21), calls=%async_computation | async-start | bytes 1572864 | tf_op jit(solution)/shard_map/all_to_all | solution.py:54
  69.7 0.0 copy-start.1
  69.7 0.0 copy-start.4
  69.7 4.9 %fusion.19 = f32[96,4096]{1,0:T(8,128)S(1)} fusion(bf16[1024,4096]{1,0:T(8,128)(2,1)} %copy-done, f32[1024,96]{0,1:T(8,128)S(1)} %fusion.11), kind=kOutput, calls=%fused_computation.22 | convolution fusion | flops 805404672 | bytes 10354688 | tf_op jit(solution)/shard_map/dot_general | solution.py:57
  74.6 43.0 %fusion = f32[8,4096]{1,0:T(8,128)S(1)} fusion(f32[96,4096]{1,0:T(8,128)S(1)} %fusion.19), kind=kCustom, calls=%all-reduce-scatter | all-reduce-scatter fusion | flops 524289 | bytes 1704448
  117.6 1.3 collective-permute-start
  118.9 1.3 collective-permute-start.1
  120.2 2.2 %collective-permute-start.2 = (f32[8,4096]{1,0:T(8,128)S(1)}, f32[8,4096]{1,0:T(8,128)S(1)}, u32[]{:S(2)}, u32[]{:S(2)}) collective-permute-start(f32[8,4096]{1,0:T(8,128)S(1)} %fusion), channel_id=1, source_target_pairs={{0,3},{1,4},{2,5},{3,6},{4,7},{5,8},{6,9},{7,10},{8,11},{9,12},{10... | collective-permute-start | bytes 393224
  122.4 4.5 %collective-permute-start.3 = (f32[6,4096]{1,0:T(8,128)S(1)}, f32[6,4096]{1,0:T(8,128)S(1)}, u32[]{:S(2)}, u32[]{:S(2)}) collective-permute-start(f32[6,4096]{1,0:T(8,128)S(1)} %slice.10), channel_id=1, source_target_pairs={{0,4},{1,5},{2,6},{3,7},{4,8},{5,9},{6,10},{7,11},{8,12},{9,13},{1... | collective-permute-start | bytes 294920
  126.9 0.5 fusion.10
  127.4 57.7 %psum.7 = f32[16,96]{0,1:T(8,128)S(1)} all-reduce(f32[16,96]{0,1:T(8,128)S(1)} %fusion.10), channel_id=1, replica_groups=mesh['groups'=2,'blk'=8,'dp'=2] {'blk','dp'}, use_global_device_ids=true, to_apply=%region_3.4 | all-reduce | flops 1536 | bytes 12288 | tf_op jit(solution)/shard_map/psum | solution.py:67
  185.1 0.0 copy-done.1
  185.1 0.9 fusion.16
  186.0 0.0 copy-done.4
  186.0 0.6 dynamic-slice.4
  187.3 0.0 collective-permute-done.3
  187.3 0.0 collective-permute-done
  187.3 0.0 collective-permute-done.1
  187.3 0.0 collective-permute-done.2
  187.3 0.8 concatenate
  188.1 0.7 constant_dynamic-slice_fusion
  188.8 0.0 all-to-all-done
  188.8 0.9 copy_bitcast_fusion
  (6 shorter events, 0.1 us)
Async XLA Ops:
  47.7 3.2 %copy-start = (bf16[1024,4096]{1,0:T(8,128)(2,1)}, bf16[1024,4096]{1,0:T(8,128)(2,1)S(1)}, u32[]{:S(2)}) copy-start(bf16[1024,4096]{1,0:T(8,128)(2,1)S(1)} %multiply_convert_fusion) | copy-start | bytes 25165828
  51.0 2.7 %copy-start.2 = (s32[1024]{0:T(1024)S(1)}, s32[1024]{0:T(1024)}, u32[]{:S(2)}) copy-start(s32[1024]{0:T(1024)} %param.6) | copy-start | bytes 12292
  51.0 3.7 %copy-start.3 = (s32[1024,1]{0,1:T(1,128)S(1)}, s32[1024,1]{0,1:T(1,128)}, u32[]{:S(2)}) copy-start(s32[1024,1]{0,1:T(1,128)} %param.7) | copy-start | bytes 12292
  64.2 124.6 %all-to-all-start = ((f32[16,128,96]{1,2,0:T(8,128)}), f32[16,128,96]{1,2,0:T(8,128)S(1)}, u32[]{:S(2)}, u32[]{:S(2)}) async-start(f32[16,128,96]{1,2,0:T(8,128)} %copy.21), calls=%async_computation | async-start | bytes 1572864 | tf_op jit(solution)/shard_map/all_to_all | solution.py:54
  69.7 115.4 %copy-start.1 = (f32[16,4096]{1,0:T(8,128)S(1)}, f32[16,4096]{1,0:T(8,128)}, u32[]{:S(2)}) copy-start(f32[16,4096]{1,0:T(8,128)} %param.9) | copy-start | bytes 786436
  69.7 116.3 %copy-start.4 = (u32[32]{0:T(128)S(1)}, u32[32]{0:T(128)}, u32[]{:S(2)}) copy-start(u32[32]{0:T(128)} %constant.37) | copy-start | bytes 388
  117.6 69.7 %collective-permute-start = (f32[8,4096]{1,0:T(8,128)S(1)}, f32[8,4096]{1,0:T(8,128)S(1)}, u32[]{:S(2)}, u32[]{:S(2)}) collective-permute-start(f32[8,4096]{1,0:T(8,128)S(1)} %fusion), channel_id=1, source_target_pairs={{0,1},{1,2},{2,3},{3,4},{4,5},{5,6},{6,7},{7,8},{8,9},{9,10},{10,1... | collective-permute-start | bytes 393224
  118.9 68.4 %collective-permute-start.1 = (f32[8,4096]{1,0:T(8,128)S(1)}, f32[8,4096]{1,0:T(8,128)S(1)}, u32[]{:S(2)}, u32[]{:S(2)}) collective-permute-start(f32[8,4096]{1,0:T(8,128)S(1)} %fusion), channel_id=1, source_target_pairs={{0,2},{1,3},{2,4},{3,5},{4,6},{5,7},{6,8},{7,9},{8,10},{9,11},{10,... | collective-permute-start | bytes 393224
  120.2 67.1 %collective-permute-start.2 = (f32[8,4096]{1,0:T(8,128)S(1)}, f32[8,4096]{1,0:T(8,128)S(1)}, u32[]{:S(2)}, u32[]{:S(2)}) collective-permute-start(f32[8,4096]{1,0:T(8,128)S(1)} %fusion), channel_id=1, source_target_pairs={{0,3},{1,4},{2,5},{3,6},{4,7},{5,8},{6,9},{7,10},{8,11},{9,12},{10... | collective-permute-start | bytes 393224
  122.4 64.9 %collective-permute-start.3 = (f32[6,4096]{1,0:T(8,128)S(1)}, f32[6,4096]{1,0:T(8,128)S(1)}, u32[]{:S(2)}, u32[]{:S(2)}) collective-permute-start(f32[6,4096]{1,0:T(8,128)S(1)} %slice.10), channel_id=1, source_target_pairs={{0,4},{1,5},{2,6},{3,7},{4,8},{5,9},{6,10},{7,11},{8,12},{9,13},{1... | collective-permute-start | bytes 294920
where the time goes:
time: 190 us
  blocking collectives  136 us (72%)
  matrix products  21.6 us (11%)
  starting transfers between devices  14.8 us (8%)
  local copies, waits for them, and re-layouts  11.5 us (6%)
  other arithmetic  4.82 us (3%)
    psum x1, blocking collectives, per_device(): totals = lax.psum(class_sums, ('blk', 'dp'))  57.7 us
    unnamed x1, blocking collectives  43 us
    all_gather x1, blocking collectives, per_device(): ref_piece = lax.all_gather(references, 'blk', axis=0, tiled=True)  34.8 us
    dot_general x1, matrix products, per_device(): modulation = jnp.dot(own_onehot, ctf_table, precision=lax.Precision.HIGHEST)  9.82 us
    unnamed x4, starting transfers between devices  9.27 us
    all_to_all x1, starting transfers between devices, per_device(): lax.all_to_all(send_weights, ('blk', 'dp'), split_axis=0, concat_axis=0,...  5.49 us
    unnamed x15, local copies, waits for them, and re-layouts  5.48 us
    dot_general x1, matrix products, per_device(): lax.dot_general(weights_low, modulated, (((0,), (0,)), ((), ())), preferr...  4.87 us
  transfers between devices with their start and end apart: 5, of which 0 were waited for; matrix products, arithmetic and copies ran while one was open for 27% of the time, Pallas kernels for 0%

commit v1 on v0

--- a/solution.py
+++ b/solution.py
@@ -64,7 +64,7 @@
     class_sums = lax.dot_general(
         own_onehot, weights, (((0,), (0,)), ((), ())), precision=lax.Precision.HIGHEST
     )
-    totals = lax.psum(class_sums, ("blk", "dp"))
+    totals = jnp.sum(lax.all_gather(class_sums, ("blk", "dp")), axis=0)
     own_sums = lax.dynamic_slice_in_dim(
         totals, lax.axis_index(("blk", "dp")) * rows_mine, rows_mine, 1
     )

time: 190 us -> 150 us (0.79)
  blocking collectives: 136 us -> 95.5 us
    psum x1 -> x0, blocking collectives: 57.7 us -> none  [per_device(): totals = lax.psum(class_sums, ('blk', 'dp'))]
    all_gather x0 -> x1, blocking collectives: none -> 17.7 us  [per_device(): totals = jnp.sum(lax.all_gather(class_sums, ('blk', 'dp')), axis=0)]
  transfers between devices with their start and end apart: 5 -> 5, of which waited for: 0 -> 0; matrix products, arithmetic and copies ran while one was open for 27% -> 34% of each run, Pallas kernels for 0% -> 0%
where the time goes in v1:
time: 150 us
  blocking collectives  95.5 us (64%)
  matrix products  21.9 us (15%)
  starting transfers between devices  14.8 us (10%)
  local copies, waits for them, and re-layouts  11.5 us (8%)
  other arithmetic  4.85 us (3%)
  between operations  1.53 us (1%)
    unnamed x1, blocking collectives  43 us
    all_gather x1, blocking collectives, per_device(): ref_piece = lax.all_gather(references, 'blk', axis=0, tiled=True)  34.8 us
    all_gather x1, blocking collectives, per_device(): totals = jnp.sum(lax.all_gather(class_sums, ('blk', 'dp')), axis=0)  17.7 us
    dot_general x1, matrix products, per_device(): modulation = jnp.dot(own_onehot, ctf_table, precision=lax.Precision.HIGHEST)  9.82 us
    unnamed x4, starting transfers between devices  9.27 us
    all_to_all x1, starting transfers between devices, per_device(): lax.all_to_all(send_weights, ('blk', 'dp'), split_axis=0, concat_axis=0,...  5.49 us
    unnamed x15, local copies, waits for them, and re-layouts  5.48 us
    dot_general x1, matrix products, per_device(): lax.dot_general(weights_low, modulated, (((0,), (0,)), ((), ())), preferr...  4.87 us
  transfers between devices with their start and end apart: 5, of which 0 were waited for; matrix products, arithmetic and copies ran while one was open for 34% of the time, Pallas kernels for 0%

profile of v1, /device:TPU:0, one launch (start us, length us, event | category | flops | bytes accessed | tf_op | source)
XLA Modules:
  0.0 150.0 jit_solution(15171070898131193876)
XLA Ops:
  0.6 34.8 %all-gather.1 = bf16[8,12,4096]{2,1,0:T(8,128)(2,1)S(1)} all-gather(bf16[1,12,4096]{2,1,0:T(8,128)(2,1)} %bitcast.42), channel_id=1, replica_groups=mesh['groups'=2,'blk'=8,'dp'=2] {'blk'}, dimensions={0}, use_global_device_ids=true | all-gather | bytes 884736 | tf_op jit(solution)/shard_map/all_gather | solution.py:36
  35.4 0.2 reshape.39
  35.6 2.3 %fusion.5 = f32[16,96]{1,0:T(8,128)S(1)} fusion(bf16[96,4096]{1,0:T(8,128)(2,1)S(1)} %reshape.39, f32[16,4096]{1,0:T(8,128)} %param.9), kind=kOutput, calls=%fused_computation.7 | convolution fusion | flops 76350976 | bytes 1054720 | tf_op jit(solution)/shard_map/dot_general | solution.py:41
  37.9 9.8 %multiply_convert_fusion = bf16[1024,4096]{1,0:T(8,128)(2,1)S(1)} fusion(bf16[1024,4096]{1,0:T(8,128)(2,1)} %param.5, f32[16,4096]{1,0:T(8,128)} %param.9, s32[1024]{0:T(1024)} %param.6), kind=kOutput, calls=%fused_computation.1 | convolution fusion | flops 817905664 | bytes 17043456 | tf_op jit(solution)/shard_map/dot_general | solution.py:27
  47.7 0.0 copy-start
  47.7 3.2 %copy-done = bf16[1024,4096]{1,0:T(8,128)(2,1)} copy-done((bf16[1024,4096]{1,0:T(8,128)(2,1)}, bf16[1024,4096]{1,0:T(8,128)(2,1)S(1)}, u32[]{:S(2)}) %copy-start) | copy-done | bytes 8388632
  51.0 0.0 copy-start.2
  51.0 0.0 copy-start.3
  51.0 2.7 %fusion.30 = f32[1024,96]{0,1:T(8,128)S(1)} fusion(bf16[1024,4096]{1,0:T(8,128)(2,1)S(1)} %multiply_convert_fusion, bf16[96,4096]{1,0:T(8,128)(2,1)S(1)} %reshape.39), kind=kOutput, calls=%fused_computation.38 | convolution fusion | flops 805306368 | bytes 9568256 | tf_op jit(solution)/shard_map/dot_general | solution.py:37
  53.7 0.0 copy-done.2
  53.7 0.6 fusion.29
  54.3 0.1 fusion.12
  54.3 0.1 fusion.11
  54.4 0.2 copy.20
  54.6 0.0 copy-done.3
  54.6 4.5 %reduce-window.6 = s32[16,8,128]{2,1,0:T(8,128)S(1)} reduce-window(s32[16,8,128]{2,1,0:T(8,128)S(1)} %fusion.26, s32[]{:T(128)} %constant.6.clone.1), window={size=1x1x128 pad=0_0x0_0x127_0}, to_apply=%region_4.5 | reduce-window | flops 2080768 | bytes 131076 | tf_op jit(solution)/shard_map/reduce-window
  59.2 0.1 slice.8
  59.2 0.1 copy.18
  59.4 0.1 copy.19
  59.5 0.1 broadcast_add_fusion
  59.6 3.3 %scatter_custom_fusion = f32[2048,96]{1,0:T(8,128)S(1)} fusion(s32[1024]{0:T(1024)S(1)} %bitcast.47, f32[1024,96]{1,0:T(8,128)S(1)} %copy.20, f32[]{:T(128)} %constant.15.clone.1), kind=kCustom, calls=%fused_computation.9 | custom fusion | bytes 786436 | tf_op jit(solution)/shard_map/scatter | solution.py:53
  63.0 1.2 copy.21
  64.2 5.5 %all-to-all-start = ((f32[16,128,96]{1,2,0:T(8,128)}), f32[16,128,96]{1,2,0:T(8,128)S(1)}, u32[]{:S(2)}, u32[]{:S(2)}) async-start(f32[16,128,96]{1,2,0:T(8,128)} %copy.21), calls=%async_computation | async-start | bytes 1572864 | tf_op jit(solution)/shard_map/all_to_all | solution.py:54
  69.7 0.0 copy-start.1
  69.7 0.0 copy-start.4
  69.7 4.9 %fusion.21 = f32[96,4096]{1,0:T(8,128)S(1)} fusion(bf16[1024,4096]{1,0:T(8,128)(2,1)} %copy-done, f32[1024,96]{0,1:T(8,128)S(1)} %fusion.11), kind=kOutput, calls=%fused_computation.23 | convolution fusion | flops 805404672 | bytes 10354688 | tf_op jit(solution)/shard_map/dot_general | solution.py:57
  74.6 43.0 %fusion = f32[8,4096]{1,0:T(8,128)S(1)} fusion(f32[96,4096]{1,0:T(8,128)S(1)} %fusion.21), kind=kCustom, calls=%all-reduce-scatter | all-reduce-scatter fusion | flops 524289 | bytes 1704448
  117.6 1.3 collective-permute-start
  118.9 1.3 collective-permute-start.1
  120.2 2.2 %collective-permute-start.2 = (f32[8,4096]{1,0:T(8,128)S(1)}, f32[8,4096]{1,0:T(8,128)S(1)}, u32[]{:S(2)}, u32[]{:S(2)}) collective-permute-start(f32[8,4096]{1,0:T(8,128)S(1)} %fusion), channel_id=1, source_target_pairs={{0,3},{1,4},{2,5},{3,6},{4,7},{5,8},{6,9},{7,10},{8,11},{9,12},{10... | collective-permute-start | bytes 393224
  122.4 4.5 %collective-permute-start.3 = (f32[6,4096]{1,0:T(8,128)S(1)}, f32[6,4096]{1,0:T(8,128)S(1)}, u32[]{:S(2)}, u32[]{:S(2)}) collective-permute-start(f32[6,4096]{1,0:T(8,128)S(1)} %slice.10), channel_id=1, source_target_pairs={{0,4},{1,5},{2,6},{3,7},{4,8},{5,9},{6,10},{7,11},{8,12},{9,13},{1... | collective-permute-start | bytes 294920
  126.9 0.6 fusion.13
  127.5 17.7 %all-gather = f32[256,96]{1,0:T(8,128)S(1)} all-gather(f32[16,96]{1,0:T(8,128)S(1)} %fusion.13), channel_id=2, replica_groups=mesh['groups'=2,'blk'=8,'dp'=2] {'blk','dp'}, dimensions={0}, use_global_device_ids=true | all-gather | bytes 104448 | tf_op jit(solution)/shard_map/all_gather | solution.py:67
  145.3 0.0 copy-done.1
  145.3 1.0 fusion.18
  146.3 0.0 copy-done.4
  146.3 0.6 dynamic-slice.4
  147.6 0.0 collective-permute-done.3
  147.6 0.0 collective-permute-done
  147.6 0.0 collective-permute-done.1
  147.6 0.0 collective-permute-done.2
  147.6 0.8 concatenate
  148.4 0.7 constant_dynamic-slice_fusion
  149.1 0.0 all-to-all-done
  149.1 0.9 copy_bitcast_fusion
  (7 shorter events, 0.1 us)
Async XLA Ops:
  47.7 3.2 %copy-start = (bf16[1024,4096]{1,0:T(8,128)(2,1)}, bf16[1024,4096]{1,0:T(8,128)(2,1)S(1)}, u32[]{:S(2)}) copy-start(bf16[1024,4096]{1,0:T(8,128)(2,1)S(1)} %multiply_convert_fusion) | copy-start | bytes 25165828
  51.0 2.7 %copy-start.2 = (s32[1024]{0:T(1024)S(1)}, s32[1024]{0:T(1024)}, u32[]{:S(2)}) copy-start(s32[1024]{0:T(1024)} %param.6) | copy-start | bytes 12292
  51.0 3.7 %copy-start.3 = (s32[1024,1]{0,1:T(1,128)S(1)}, s32[1024,1]{0,1:T(1,128)}, u32[]{:S(2)}) copy-start(s32[1024,1]{0,1:T(1,128)} %param.7) | copy-start | bytes 12292
  64.2 84.9 %all-to-all-start = ((f32[16,128,96]{1,2,0:T(8,128)}), f32[16,128,96]{1,2,0:T(8,128)S(1)}, u32[]{:S(2)}, u32[]{:S(2)}) async-start(f32[16,128,96]{1,2,0:T(8,128)} %copy.21), calls=%async_computation | async-start | bytes 1572864 | tf_op jit(solution)/shard_map/all_to_all | solution.py:54
  69.7 75.6 %copy-start.1 = (f32[16,4096]{1,0:T(8,128)S(1)}, f32[16,4096]{1,0:T(8,128)}, u32[]{:S(2)}) copy-start(f32[16,4096]{1,0:T(8,128)} %param.9) | copy-start | bytes 786436
  69.7 76.6 %copy-start.4 = (u32[32]{0:T(128)S(1)}, u32[32]{0:T(128)}, u32[]{:S(2)}) copy-start(u32[32]{0:T(128)} %constant.37) | copy-start | bytes 388
  117.6 30.0 %collective-permute-start = (f32[8,4096]{1,0:T(8,128)S(1)}, f32[8,4096]{1,0:T(8,128)S(1)}, u32[]{:S(2)}, u32[]{:S(2)}) collective-permute-start(f32[8,4096]{1,0:T(8,128)S(1)} %fusion), channel_id=1, source_target_pairs={{0,1},{1,2},{2,3},{3,4},{4,5},{5,6},{6,7},{7,8},{8,9},{9,10},{10,1... | collective-permute-start | bytes 393224
  118.9 28.7 %collective-permute-start.1 = (f32[8,4096]{1,0:T(8,128)S(1)}, f32[8,4096]{1,0:T(8,128)S(1)}, u32[]{:S(2)}, u32[]{:S(2)}) collective-permute-start(f32[8,4096]{1,0:T(8,128)S(1)} %fusion), channel_id=1, source_target_pairs={{0,2},{1,3},{2,4},{3,5},{4,6},{5,7},{6,8},{7,9},{8,10},{9,11},{10,... | collective-permute-start | bytes 393224
  120.2 27.4 %collective-permute-start.2 = (f32[8,4096]{1,0:T(8,128)S(1)}, f32[8,4096]{1,0:T(8,128)S(1)}, u32[]{:S(2)}, u32[]{:S(2)}) collective-permute-start(f32[8,4096]{1,0:T(8,128)S(1)} %fusion), channel_id=1, source_target_pairs={{0,3},{1,4},{2,5},{3,6},{4,7},{5,8},{6,9},{7,10},{8,11},{9,12},{10... | collective-permute-start | bytes 393224
  122.4 25.1 %collective-permute-start.3 = (f32[6,4096]{1,0:T(8,128)S(1)}, f32[6,4096]{1,0:T(8,128)S(1)}, u32[]{:S(2)}, u32[]{:S(2)}) collective-permute-start(f32[6,4096]{1,0:T(8,128)S(1)} %slice.10), channel_id=1, source_target_pairs={{0,4},{1,5},{2,6},{3,7},{4,8},{5,9},{6,10},{7,11},{8,12},{9,13},{1... | collective-permute-start | bytes 294920
